TPU v7x, 32 devices: a whole 2x2x4 slice. The times are simulated.
32 devices in a mesh: row: 4 (over y, x), seq: 2 (over core), head: 4 (over z).
Axes of the slice: x: 2, y: 2, z: 4, core: 2. Of those that a mesh axis runs over, the one named last changes fastest.
Arguments:
- inputs: bfloat16 [16, 1024, 768], P('row', ('seq', 'head')), may hold values from -6 to 6
- segment_ids: int32 [16, 1024], P('row', 'seq'), may hold values from 0 to 63, as said below
- w_project: bfloat16 [12, 3, 64, 768], P('head'), may hold values from -0.375 to 0.375
- proj_bias: bfloat16 [2, 768], P(None, 'head'), may hold values from -3 to 3
- conv_taps: bfloat16 [12, 33], P('head'), may hold values from -0.375 to 0.375
- w_output: bfloat16 [768, 768], P('head'), may hold values from -0.375 to 0.375
- out_bias: bfloat16 [768], replicated, may hold values from -1.75 to 1.75
- norm_attn: bfloat16 [2, 768], replicated, may hold values from 0.25 to 1.75
- w_hidden: bfloat16 [768, 3072], P(None, 'head'), may hold values from -0.21875 to 0.21875
- hid_bias: bfloat16 [3072], P('head'), may hold values from -3 to 3
- w_down: bfloat16 [3072, 768], P('head'), may hold values from -0.15625 to 0.15625
- down_bias: bfloat16 [768], replicated, may hold values from -1.75 to 1.75
- norm_ffn: bfloat16 [2, 768], replicated, may hold values from 0.25 to 1.75
- cotangent: bfloat16 [16, 1024, 768], P('row', ('seq', 'head')), may hold values from -6 to 6
Outputs:
- layer_out: bfloat16 [16, 1024, 768], P('row', ('seq', 'head'))
- grad_inputs: bfloat16 [16, 1024, 768], P('row', ('seq', 'head'))
- grad_project: float32 [12, 3, 64, 768], P('head', None, None, ('row', 'seq'))
- grad_projbias: float32 [2, 768], P(None, 'head')
- grad_conv: float32 [12, 33], P('head')
- grad_output: float32 [768, 768], P('head', ('row', 'seq'))
- grad_outbias: float32 [768], P('head')
- grad_normattn: float32 [2, 768], P(None, 'head')
- grad_hidden: float32 [768, 3072], P(('row', 'seq'), 'head')
- grad_hidbias: float32 [3072], P('head')
- grad_down: float32 [3072, 768], P('head', ('row', 'seq'))
- grad_downbias: float32 [768], P('head')
- grad_normffn: float32 [2, 768], P(None, 'head')
Inputs may be any that keep to these rules, and one draw needn't show every extreme that they name: `segment_ids`: along each document the ids never fall; every id occurs, on 1 to 31 consecutive positions, both extremes reached in every document; segment i ends fewer than 16 positions after position (i + 1) * 16.
All inputs are finite; a program needn't handle non-finite values.
Results may differ from a plain program's by a relative error of at most 0.024.
The roundings to bfloat16 on the way count: a program that leaves them out, or rounds other values in their place, can miss the bound.
Values may be sent and summed in bfloat16 or wider, within the bound.
A program may use at most 192 MiB of HBM per device.

v0:
```python
import jax
import jax.numpy as jnp
from jax import lax
from jax.sharding import PartitionSpec as P

HEAD_DIM = 64
LANDMARKS = 64
CONV_TAPS = 33
NEWTON_STEPS = 6


EPS = 1e-05
HIGH_ACCURACY = lax.Precision.HIGHEST


def combined_all(part, axis, combine):
    gathered = jax.tree.map(lambda a: lax.all_gather(a, axis), part)

    def take(source):
        return jax.tree.map(lambda a: lax.dynamic_index_in_dim(a, source, 0, False), gathered)

    return lax.fori_loop(
        1, lax.axis_size(axis), lambda source, state: combine(state, take(source)), take(0)
    )


def padded(cells, sides, width):
    for axis, dim in sides:
        count = lax.axis_size(axis)
        ends = count - 1
        head = lax.slice_in_dim(cells, 0, width, axis=dim)
        tail = lax.slice_in_dim(cells, cells.shape[dim] - width, cells.shape[dim], axis=dim)
        cells = jnp.concatenate(
            [
                lax.ppermute(tail, axis, [(i, (i + 1) % count) for i in range(ends)]),
                cells,
                lax.ppermute(head, axis, [((i + 1) % count, i) for i in range(ends)]),
            ],
            axis=dim,
        )
    return cells


def newton_schulz_inverse(kernel):
    order_size = kernel.shape[-1]
    identity = jnp.eye(order_size, dtype=jnp.float32)
    estimate = jnp.swapaxes(kernel, -1, -2) / order_size
    for repeat in range(NEWTON_STEPS):
        product = jnp.einsum("...ij,...jk->...ik", kernel, estimate, precision=HIGH_ACCURACY)
        nested = 7.0 * identity - product
        nested = 15.0 * identity - jnp.einsum(
            "...ij,...jk->...ik", product, nested, precision=HIGH_ACCURACY
        )
        nested = 13.0 * identity - jnp.einsum(
            "...ij,...jk->...ik", product, nested, precision=HIGH_ACCURACY
        )
        estimate = 0.25 * jnp.einsum(
            "...ij,...jk->...ik", estimate, nested, precision=HIGH_ACCURACY
        )
    return estimate


def exact_gelu(pre_act):
    return jax.nn.gelu(pre_act, approximate=False)


def merge_softmax(former, latter):
    top_one, total_one, pooled_one = former
    top_two, total_two, pooled_two = latter
    top_new = jnp.maximum(top_one, top_two)
    factor_one = jnp.exp(top_one - top_new)
    factor_two = jnp.exp(top_two - top_new)
    return (
        top_new,
        total_one * factor_one + total_two * factor_two,
        pooled_one * factor_one[..., None] + pooled_two * factor_two[..., None],
    )


def gather_rows(partial_value):
    return lax.all_gather(partial_value, "head", axis=1, tiled=True)


def sum_rows(partial_value):
    return lax.psum(partial_value.astype(jnp.bfloat16), "head").astype(jnp.float32)


def sum_shares(partial_value):
    return lax.psum_scatter(
        partial_value.astype(jnp.bfloat16), "head", scatter_dimension=1, tiled=True
    ).astype(jnp.float32)


def norm_apply(residual, gain_row, shift_row):
    former = jnp.mean(residual, axis=-1)
    centered_raw = residual - former[..., None]
    variance = jnp.mean(centered_raw * centered_raw, axis=-1)
    inv_dev = lax.rsqrt(variance + EPS)
    centered = centered_raw * inv_dev[..., None]
    return (centered * gain_row + shift_row, centered, inv_dev)


def norm_back(incoming, centered, inv_dev, gain_row):
    scaled = incoming * gain_row
    former = jnp.mean(scaled, axis=-1)
    latter = jnp.mean(scaled * centered, axis=-1)
    return inv_dev[..., None] * (scaled - former[..., None] - centered * latter[..., None])


def norm_grads(incoming, centered):
    return jnp.stack([jnp.sum(incoming * centered, axis=(0, 1)), jnp.sum(incoming, axis=(0, 1))])


def on_device(
    inputs,
    segment_ids,
    w_project,
    proj_bias,
    conv_taps,
    w_output,
    out_bias,
    norm_attn,
    w_hidden,
    hid_bias,
    w_down,
    down_bias,
    norm_ffn,
    cotangent,
):
    seqs_here, rows_own, model_width = inputs.shape
    heads_here = w_project.shape[0]
    width_here = heads_here * HEAD_DIM
    half_taps = CONV_TAPS // 2
    scores_factor = HEAD_DIM ** (-0.5)
    head_place = lax.axis_index("head")
    head_start = head_place * width_here
    row_start = head_place * rows_own

    def own_rows(source):
        return lax.dynamic_slice_in_dim(source, row_start, rows_own, axis=1)

    full_input = gather_rows(inputs)
    tokens_here = full_input.shape[1]

    def split_heads(source, row_count):
        return source.reshape(seqs_here, row_count, heads_here, HEAD_DIM)

    mixed_proj = jnp.einsum(
        "ste,hcfe->csthf", full_input, w_project, preferred_element_type=jnp.float32
    )
    mixed_proj = mixed_proj.reshape(3, seqs_here, tokens_here, width_here)
    query_tokens = (mixed_proj[0] + proj_bias[0]).astype(jnp.bfloat16)
    key_tokens = mixed_proj[1].astype(jnp.bfloat16)
    value_tokens = (mixed_proj[2] + proj_bias[1]).astype(jnp.bfloat16)
    segment_membership = (
        segment_ids[:, :, None] == jnp.arange(LANDMARKS, dtype=jnp.int32)[None, None, :]
    )
    member_low = segment_membership.astype(jnp.bfloat16)
    member_wide = segment_membership.astype(jnp.float32)
    query_sums = jnp.einsum(
        "stm,std->smd", member_low, query_tokens, preferred_element_type=jnp.float32
    )
    key_sums = jnp.einsum(
        "stm,std->smd", member_low, key_tokens, preferred_element_type=jnp.float32
    )
    segment_count = jnp.sum(member_wide, axis=1)
    query_sums, key_sums, segment_count = lax.psum((query_sums, key_sums, segment_count), "seq")
    query_landmarks = (query_sums / segment_count[:, :, None]).astype(jnp.bfloat16)
    key_landmarks = (key_sums / segment_count[:, :, None]).astype(jnp.bfloat16)
    q_heads = split_heads(query_tokens, tokens_here)
    k_heads = split_heads(key_tokens, tokens_here)
    v_heads = split_heads(value_tokens, tokens_here)
    ql_heads = split_heads(query_landmarks, LANDMARKS)
    kl_heads = split_heads(key_landmarks, LANDMARKS)
    ql_wide = ql_heads.astype(jnp.float32)
    kl_wide = kl_heads.astype(jnp.float32)
    v_wide = v_heads.astype(jnp.float32)
    first_scores = (
        jnp.einsum("sthd,smhd->shtm", q_heads, kl_heads, preferred_element_type=jnp.float32)
        * scores_factor
    )
    first_kernel = jax.nn.softmax(first_scores, axis=-1)
    kern_low = first_kernel.astype(jnp.bfloat16)
    score_two = (
        jnp.einsum("smhd,snhd->shmn", ql_heads, kl_heads, preferred_element_type=jnp.float32)
        * scores_factor
    )
    second_kernel = jax.nn.softmax(score_two, axis=-1)
    inverse, inverse_back = jax.vjp(newton_schulz_inverse, second_kernel)
    third_scores = (
        jnp.einsum("smhd,sthd->shmt", ql_heads, k_heads, preferred_element_type=jnp.float32)
        * scores_factor
    )
    top_local = jnp.max(third_scores, axis=-1)
    weight_local = jnp.exp(third_scores - top_local[..., None])
    total_local = jnp.sum(weight_local, axis=-1)
    pooled_local = jnp.einsum("shmt,sthd->shmd", weight_local, v_wide, precision=HIGH_ACCURACY)
    top_all, total_all, pooled_all = combined_all(
        (top_local, total_local, pooled_local), "seq", merge_softmax
    )
    segment_means = pooled_all / total_all[..., None]
    log_total = top_all + jnp.log(total_all)
    reduced_mixer = jnp.einsum(
        "shmn,shnd->shmd", inverse, segment_means, precision=HIGH_ACCURACY
    ).astype(jnp.bfloat16)
    landmark_output = jnp.einsum(
        "shtm,shmd->sthd", kern_low, reduced_mixer, preferred_element_type=jnp.float32
    )
    value_rim = padded(value_tokens, (("seq", 1),), half_taps)
    rim_heads = split_heads(value_rim.astype(jnp.float32), tokens_here + 2 * half_taps)
    tap_wide = conv_taps.astype(jnp.float32)
    conv_out = jnp.zeros((seqs_here, tokens_here, heads_here, HEAD_DIM), jnp.float32)
    for offset in range(CONV_TAPS):
        conv_out = (
            conv_out
            + tap_wide[:, offset][None, None, :, None] * rim_heads[:, offset : offset + tokens_here]
        )
    attended = (
        (landmark_output + conv_out)
        .reshape(seqs_here, tokens_here, width_here)
        .astype(jnp.bfloat16)
    )
    out_part = jnp.dot(attended, w_output, preferred_element_type=jnp.float32)
    gain_one = norm_attn[0].astype(jnp.float32)
    shift_one = norm_attn[1].astype(jnp.float32)
    gain_two = norm_ffn[0].astype(jnp.float32)
    shift_two = norm_ffn[1].astype(jnp.float32)
    resid_one = full_input.astype(jnp.float32) + sum_rows(out_part) + out_bias.astype(jnp.float32)
    normed_one, centered_one, inv_one = norm_apply(resid_one, gain_one, shift_one)
    normed_low = normed_one.astype(jnp.bfloat16)
    hidden_pre = jnp.dot(
        normed_low, w_hidden, preferred_element_type=jnp.float32
    ) + hid_bias.astype(jnp.float32)
    active, gelu_back = jax.vjp(exact_gelu, hidden_pre)
    active_low = active.astype(jnp.bfloat16)
    down_part = jnp.dot(active_low, w_down, preferred_element_type=jnp.float32)
    resid_two = normed_one + sum_rows(down_part) + down_bias.astype(jnp.float32)
    normed_two, centered_two, inv_two = norm_apply(resid_two, gain_two, shift_two)
    layer_out = own_rows(normed_two).astype(jnp.bfloat16)
    grad_y = gather_rows(cotangent).astype(jnp.float32)
    grad_two = norm_back(grad_y, centered_two, inv_two, gain_two)
    norm_ffn_grad = norm_grads(grad_y, centered_two)
    down_low = grad_two.astype(jnp.bfloat16)
    down_bias_grad = jnp.sum(down_low, axis=(0, 1), dtype=jnp.float32)
    w_down_grad = jnp.einsum(
        "stf,ste->fe", active_low, down_low, preferred_element_type=jnp.float32
    )
    grad_active = jnp.einsum("ste,fe->stf", down_low, w_down, preferred_element_type=jnp.float32)
    grad_pre = gelu_back(grad_active)[0].astype(jnp.bfloat16)
    hid_bias_grad = jnp.sum(grad_pre, axis=(0, 1), dtype=jnp.float32)
    w_hidden_grad = jnp.einsum(
        "ste,stf->ef", normed_low, grad_pre, preferred_element_type=jnp.float32
    )
    back_part = jnp.einsum("stf,ef->ste", grad_pre, w_hidden, preferred_element_type=jnp.float32)
    grad_in = grad_two + sum_rows(back_part)
    grad_one = norm_back(grad_in, centered_one, inv_one, gain_one)
    norm_attn_grad = norm_grads(grad_in, centered_one)
    out_low = grad_one.astype(jnp.bfloat16)
    out_bias_grad = jnp.sum(out_low, axis=(0, 1), dtype=jnp.float32)
    norm_stack = jnp.concatenate(
        [norm_ffn_grad, norm_attn_grad, down_bias_grad[None, :], out_bias_grad[None, :]], axis=0
    )
    norm_stack = lax.dynamic_slice_in_dim(
        norm_stack, head_start, width_here, axis=norm_stack.ndim - 1
    )
    resid_grad = own_rows(grad_one)
    norm_ffn_grad = norm_stack[0:2]
    norm_attn_grad = norm_stack[2:4]
    down_bias_grad = norm_stack[4]
    out_bias_grad = norm_stack[5]
    w_output_grad = jnp.einsum("std,ste->de", attended, out_low, preferred_element_type=jnp.float32)
    grad_att = jnp.einsum(
        "ste,de->std", out_low, w_output, preferred_element_type=jnp.float32
    ).astype(jnp.bfloat16)
    grad_heads = split_heads(grad_att, tokens_here)
    mixer_part = jnp.einsum(
        "shtm,sthd->shmd", kern_low, grad_heads, preferred_element_type=jnp.float32
    )
    kern_grad = jnp.einsum(
        "sthd,shmd->shtm", grad_heads, reduced_mixer, preferred_element_type=jnp.float32
    )
    score_grad = first_kernel * (
        kern_grad - jnp.sum(first_kernel * kern_grad, axis=-1, keepdims=True)
    )
    score_low = score_grad.astype(jnp.bfloat16)
    query_grad = (
        jnp.einsum("shtm,smhd->sthd", score_low, kl_heads, preferred_element_type=jnp.float32)
        * scores_factor
    )
    kl_part = (
        jnp.einsum("shtm,sthd->smhd", score_low, q_heads, preferred_element_type=jnp.float32)
        * scores_factor
    )
    mixer_grad, kl_grad_one = (
        lax.psum(mixer_part.astype(jnp.bfloat16), "seq").astype(jnp.float32),
        lax.psum(kl_part.astype(jnp.bfloat16), "seq").astype(jnp.float32),
    )
    inverse_grad = jnp.einsum("shmd,shnd->shmn", mixer_grad, segment_means, precision=HIGH_ACCURACY)
    pooled_grad = jnp.einsum("shmn,shmd->shnd", inverse, mixer_grad, precision=HIGH_ACCURACY)
    kern_two_grad = inverse_back(inverse_grad)[0]
    score_two_grad = second_kernel * (
        kern_two_grad - jnp.sum(second_kernel * kern_two_grad, axis=-1, keepdims=True)
    )
    ql_grad_two = (
        jnp.einsum("shmn,snhd->smhd", score_two_grad, kl_wide, precision=HIGH_ACCURACY)
        * scores_factor
    )
    kl_grad_two = (
        jnp.einsum("shmn,smhd->snhd", score_two_grad, ql_wide, precision=HIGH_ACCURACY)
        * scores_factor
    )
    third_kernel = jnp.exp(third_scores - log_total[..., None])
    kern_three_grad = jnp.einsum("shmd,sthd->shmt", pooled_grad, v_wide, precision=HIGH_ACCURACY)
    row_dot = jnp.sum(pooled_grad * segment_means, axis=-1, keepdims=True)
    score_three_low = (third_kernel * (kern_three_grad - row_dot)).astype(jnp.bfloat16)
    ql_part = (
        jnp.einsum("shmt,sthd->smhd", score_three_low, k_heads, preferred_element_type=jnp.float32)
        * scores_factor
    )
    key_grad = (
        jnp.einsum("shmt,smhd->sthd", score_three_low, ql_heads, preferred_element_type=jnp.float32)
        * scores_factor
    )
    value_grad = jnp.einsum("shmt,shmd->sthd", third_kernel, pooled_grad, precision=HIGH_ACCURACY)
    ql_grad = lax.psum(ql_part.astype(jnp.bfloat16), "seq").astype(jnp.float32) + ql_grad_two
    kl_grad = kl_grad_one + kl_grad_two
    per_count = 1.0 / segment_count[:, :, None]
    ql_spread = ql_grad.reshape(seqs_here, LANDMARKS, width_here) * per_count
    kl_spread = kl_grad.reshape(seqs_here, LANDMARKS, width_here) * per_count
    query_grad = query_grad + split_heads(
        jnp.einsum("stm,smd->std", member_wide, ql_spread, precision=HIGH_ACCURACY), tokens_here
    )
    key_grad = key_grad + split_heads(
        jnp.einsum("stm,smd->std", member_wide, kl_spread, precision=HIGH_ACCURACY), tokens_here
    )
    grad_rim = padded(grad_att, (("seq", 1),), half_taps)
    grad_rim_heads = split_heads(grad_rim.astype(jnp.float32), tokens_here + 2 * half_taps)
    grad_wide = grad_heads.astype(jnp.float32)
    tap_list = []
    for offset in range(CONV_TAPS):
        start_at = 2 * half_taps - offset
        value_grad = (
            value_grad
            + tap_wide[:, offset][None, None, :, None]
            * grad_rim_heads[:, start_at : start_at + tokens_here]
        )
        tap_list.append(
            jnp.sum(grad_wide * rim_heads[:, offset : offset + tokens_here], axis=(0, 1, 3))
        )
    taps_grad = jnp.stack(tap_list, axis=1)
    grads_qkv = jnp.stack([query_grad, key_grad, value_grad], axis=2).astype(jnp.bfloat16)
    proj_bias_grad = jnp.sum(grads_qkv[:, :, 0::2], axis=(0, 1), dtype=jnp.float32).reshape(
        2, width_here
    )
    w_project_grad = jnp.einsum(
        "stchf,ste->hcfe", grads_qkv, full_input, preferred_element_type=jnp.float32
    )
    input_part = jnp.einsum(
        "stchf,hcfe->ste", grads_qkv, w_project, preferred_element_type=jnp.float32
    )
    input_grad = (sum_shares(input_part) + resid_grad).astype(jnp.bfloat16)
    small_sums = lax.psum(
        (
            proj_bias_grad,
            taps_grad,
            out_bias_grad,
            norm_attn_grad,
            hid_bias_grad,
            down_bias_grad,
            norm_ffn_grad,
        ),
        ("row", "seq"),
    )
    large_sums = (
        lax.psum_scatter(w_project_grad, ("row", "seq"), scatter_dimension=3, tiled=True),
        lax.psum_scatter(w_output_grad, ("row", "seq"), scatter_dimension=1, tiled=True),
        lax.psum_scatter(w_hidden_grad, ("row", "seq"), scatter_dimension=0, tiled=True),
        lax.psum_scatter(w_down_grad, ("row", "seq"), scatter_dimension=1, tiled=True),
    )
    return (
        layer_out,
        input_grad,
        large_sums[0],
        small_sums[0],
        small_sums[1],
        large_sums[1],
        small_sums[2],
        small_sums[3],
        large_sums[2],
        small_sums[4],
        large_sums[3],
        small_sums[5],
        small_sums[6],
    )


def solution(mesh):
    in_specs = (
        P("row", ("seq", "head"), None),
        P("row", "seq"),
        P("head", None, None, None),
        P(None, "head"),
        P("head", None),
        P("head", None),
        P(),
        P(),
        P(None, "head"),
        P("head"),
        P("head", None),
        P(),
        P(),
        P("row", ("seq", "head"), None),
    )
    out_specs = (
        P("row", ("seq", "head"), None),
        P("row", ("seq", "head"), None),
        P("head", None, None, ("row", "seq")),
        P(None, "head"),
        P("head", None),
        P("head", ("row", "seq")),
        P("head"),
        P(None, "head"),
        P(("row", "seq"), "head"),
        P("head"),
        P("head", ("row", "seq")),
        P("head"),
        P(None, "head"),
    )
    return jax.shard_map(
        on_device, mesh=mesh, in_specs=in_specs, out_specs=out_specs, check_vma=False
    )
```

profile of v0, /device:TPU:0, one launch (start us, length us, event | category | flops | bytes accessed | tf_op | source)
XLA Modules:
  0.0 1002.7 jit_solution(16326339202929278498)
XLA Ops:
  10.4 2.6 psum.113
  17.0 58.7 %all-gather.6.cloned.1.call-done = bf16[4,512,768]{2,1,0:T(8,128)(2,1)} async-done(((bf16[4,128,768]{2,1,0:T(8,128)(2,1)}), bf16[4,512,768]{2,1,0:T(8,128)(2,1)}) %all-gather.6.cloned.1.call-update) | async-done | bytes 3145744 | tf_op jit(solution)/shard_map/all_gather | solution.py:81
  75.8 4.2 fusion.21
  89.3 2.9 fusion.97
  93.6 14.1 %all-reduce.18.cloned.1.call-done = (f32[4,64,192]{2,1,0:T(8,128)}, f32[4,64,192]{2,1,0:T(8,128)}) async-done(((f32[4,64,192]{2,1,0:T(8,128)}, f32[4,64,192]{2,1,0:T(8,128)}), (f32[4,64,192]{2,1,0:T(8,128)}, f32[4,64,192]{2,1,0:T(8,128)})) %all-reduce.18.cloned.1.call-update) | async-done | bytes 393232 | tf_op jit(solution)/shard_map/psum | solution.py:167
  117.5 2.6 all-gather
  144.2 3.6 fusion.252
  154.2 13.6 %fusion.96 = bf16[4,512,3,64]{1,3,0,2:T(8,128)(2,1)S(1)} fusion(f32[4,544,3,64]{1,3,0,2:T(8,128)S(1)} %maximum_convert_fusion, bf16[4,3,512,64]{2,3,1,0:T(8,128)(2,1)S(1)} %fusion.220, f32[3]{0:T(128)S(1)} %copy-done.180, f32[3]{0:T(128)S(1)} %copy-done.182, f32[3]{0:T(128)S(1)} %copy-done.184, f32[3]{0:T(128)S(1)} %copy-done.186, f32[3]{0:T(128)S(1)} %copy-done.188, ...), kind=kOutput, calls=%fused_computation.206 | convolution fusion | flops 76677120 | bytes 53576076 | tf_op jit(solution)/shard_map/shtm,shmd->sthd/dot_general | solution.py:206
  168.9 2.8 convolution_convert_fusion
  173.6 120.5 %all-reduce.10.cloned.1.call-done = bf16[4,512,768]{2,1,0:T(8,128)(2,1)} async-done(((bf16[4,512,768]{2,1,0:T(8,128)(2,1)}), bf16[4,512,768]{2,1,0:T(8,128)(2,1)}) %all-reduce.10.cloned.1.call-update) | async-done | bytes 3145744 | tf_op jit(solution)/shard_map/psum | solution.py:85
  294.1 4.1 fusion.15
  300.5 6.4 fusion.102
  306.9 15.4 %multiply_convert_fusion = (bf16[4,512,768]{2,1,0:T(8,128)(2,1)S(1)}, f32[4,512,768]{2,1,0:T(8,128)}) fusion(f32[4,512,768]{2,1,0:T(8,128)S(1)} %get-tuple-element.222, f32[768]{0:T(1024)S(1)} %copy-done.141, u8[512,768]{1,0:T(8,128)(4,1)S(1)} %get-tuple-element.95, u8[512,768]{1,0:T(8,128)(4,1)S(1)} %get-tuple-element.94), kind=kLoop, calls=%fused_computation.62 | loop fusion | flops 111673344 | bytes 16518144 | tf_op jit(solution)/shard_map/convert_element_type | solution.py:235
  324.1 4.0 convolution_convert_fusion.2
  331.8 116.5 %all-reduce.12.cloned.1.call-done = bf16[4,512,768]{2,1,0:T(8,128)(2,1)} async-done(((bf16[4,512,768]{2,1,0:T(8,128)(2,1)}), bf16[4,512,768]{2,1,0:T(8,128)(2,1)}) %all-reduce.12.cloned.1.call-update) | async-done | bytes 3145744 | tf_op jit(solution)/shard_map/psum | solution.py:85
  448.3 5.3 fusion.200
  454.8 3.5 multiply_reduce_fusion.2
  458.9 53.3 %all-gather.8.cloned.1.call-done = bf16[4,512,768]{2,1,0:T(8,128)(2,1)} async-done(((bf16[4,128,768]{2,1,0:T(8,128)(2,1)}), bf16[4,512,768]{2,1,0:T(8,128)(2,1)}) %all-gather.8.cloned.1.call-update) | async-done | bytes 3145744 | tf_op jit(solution)/shard_map/all_gather | solution.py:81
  512.2 8.9 fusion.8
  521.2 2.5 convert_reduce_fusion.3
  523.7 9.0 convert_reduce_fusion.1
  534.4 4.0 convolution_convert_fusion.1
  540.3 118.1 %all-reduce.14.cloned.1.call-done = bf16[4,512,768]{2,1,0:T(8,128)(2,1)} async-done(((bf16[4,512,768]{2,1,0:T(8,128)(2,1)}), bf16[4,512,768]{2,1,0:T(8,128)(2,1)}) %all-reduce.14.cloned.1.call-update) | async-done | bytes 3145744 | tf_op jit(solution)/shard_map/psum | solution.py:85
  658.4 10.6 %multiply_reduce_fusion = (f32[768]{0:T(1024)}, f32[4,512]{1,0:T(4,128)S(1)}, f32[4,512]{1,0:T(4,128)S(1)}, f32[768]{0:T(1024)}, f32[4,512,768]{2,1,0:T(8,128)S(1)}) fusion(f32[4,512]{1,0:T(4,128)S(1)} %add_rsqrt_fusion.1, f32[4,512]{1,0:T(4,128)S(1)} %broadcast_multiply_fusion.5, f32[768]{0:T(1024)S(1)} %copy-done.102, ...), kind=kLoop, calls=%fused_computation.55 | loop fusion | flops 33024512 | bytes 25238528 | tf_op jit(solution)/shard_map/reduce_sum | solution.py:111
  669.1 3.3 convert_reduce_fusion.2
  676.2 3.0 multiply_reduce_fusion.5
  679.3 2.4 multiply_convert_fusion.2
  687.9 8.5 all-reduce.16.cloned.1.call-done
  698.0 2.6 multiply_convert_fusion.1
  701.5 2.5 fusion.135
  704.0 5.3 convolution_bitcast_fusion.2
  709.6 2.9 copy_convert_fusion
  751.7 15.1 %fusion.109 = bf16[4,512,1,3,64]{1,4,0,3,2:T(8,128)(2,1)} fusion(f32[4,544,3,64]{1,3,0,2:T(8,128)S(1)} %copy-done.81, f32[4,3,64,512]{3,2,0,1:T(8,128)S(1)} %copy-done.15, f32[4,3,64]{2,0,1:T(4,128)S(1)} %copy-done.131, f32[3]{0:T(128)S(1)} %copy-done.181, f32[3]{0:T(128)S(1)} %copy-done.183, f32[3]{0:T(128)S(1)} %copy-done.185, f32[3]{0:T(128)S(1)} %copy-done.187, ...), kind=kOutput, calls=%fused_computation.231 | convolution fusion | flops 328728576 | bytes 54463884 | tf_op jit(solution)/shard_map/shmt,shmd->sthd/dot_general | solution.py:324
  769.9 2.4 fusion.113
  783.7 3.2 fusion.103
  787.0 5.8 copy.497
  792.8 6.0 reshape.330
  798.9 6.2 bitcast_convert_fusion
  805.8 9.0 convolution_bitcast_fusion.1
  814.8 6.9 convolution_bitcast_fusion
  822.5 2.4 fusion.93
  825.0 8.0 fusion.57
  834.7 6.0 fusion.39
  845.0 25.8 %all-reduce = (f32[2,192]{1,0:T(2,128)}, f32[3,33]{1,0:T(4,128)}, f32[192]{0:T(256)}, f32[2,192]{1,0:T(2,128)}, f32[768]{0:T(1024)}, /*index=5*/f32[192]{0:T(256)}, f32[2,192]{1,0:T(2,128)}) all-reduce(f32[2,192]{1,0:T(2,128)S(1)} %reshape.295, f32[3,33]{1,0:T(4,128)S(1)} %stack.167, ...), channel_id=1, replica_groups=mesh['row'=4,'seq'=2,'head'=4] {'row','seq'}, use_global_device_ids=true, to_apply=%region_30.31 | all-reduce | flops 2403 | bytes 19224 | tf_op jit(solution)/shard_map/psum | solution.py:362
  874.5 28.8 %reduce-scatter.10.cloned.1.call-done = bf16[4,128,768]{2,1,0:T(8,128)(2,1)} async-done(((bf16[4,512,768]{2,1,0:T(8,128)(2,1)}), bf16[4,128,768]{2,1,0:T(8,128)(2,1)}) %reduce-scatter.10.cloned.1.call-update) | async-done | bytes 786448 | tf_op jit(solution)/shard_map/reduce_scatter | solution.py:89
  903.3 2.6 add_convert_fusion.1
  906.0 43.4 %reduce-scatter.12.cloned.1.call-done = f32[96,768]{1,0:T(8,128)} async-done(((f32[768,768]{1,0:T(8,128)}), f32[96,768]{1,0:T(8,128)}) %reduce-scatter.12.cloned.1.call-update) | async-done | bytes 294928 | tf_op jit(solution)/shard_map/reduce_scatter | solution.py:377
  949.4 46.3 %reduce-scatter.14.cloned.1.call-done = f32[768,96]{0,1:T(8,128)} async-done(((f32[768,768]{0,1:T(8,128)}), f32[768,96]{0,1:T(8,128)}) %reduce-scatter.14.cloned.1.call-update) | async-done | bytes 294928 | tf_op jit(solution)/shard_map/reduce_scatter | solution.py:378
  (667 shorter events, 149.2 us)
Async XLA Ops:
  7.2 293.3 %copy-start = (bf16[768,768]{1,0:T(8,128)(2,1)S(1)}, bf16[768,768]{1,0:T(8,128)(2,1)}, u32[]{:S(2)}) copy-start(bf16[768,768]{1,0:T(8,128)(2,1)} %param.22) | copy-start | bytes 3538948
  7.2 68.6 %all-gather.6.cloned.1.call-start = ((), (), s32[]{:S(2)}) async-start(), calls=%async_computation.5 | async-start | bytes 3932160 | tf_op jit(solution)/shard_map/all_gather | solution.py:81
  7.9 99.8 %all-reduce.18.cloned.1.call-start = ((), (), s32[]{:S(2)}) async-start(), calls=%async_computation.16 | async-start | bytes 1048576 | tf_op jit(solution)/shard_map/psum | solution.py:167
  13.1 94.7 %copy-start.132 = (f32[4,64]{1,0:T(4,128)}, f32[4,64]{1,0:T(4,128)S(1)}, u32[]{:S(2)}) copy-start(f32[4,64]{1,0:T(4,128)S(1)} %psum.113) | copy-start | bytes 3076
  85.2 7.1 collective-permute-start
  86.8 5.5 collective-permute-start.1
  89.3 204.8 %all-reduce.10.cloned.1.call-start = ((), (), s32[]{:S(2)}) async-start(), calls=%async_computation.6 | async-start | bytes 6291456 | tf_op jit(solution)/shard_map/psum | solution.py:85
  109.7 16.2 %copy-start.76 = (bf16[4,64,192]{1,2,0:T(8,128)(2,1)}, bf16[4,64,192]{1,2,0:T(8,128)(2,1)S(1)}, u32[]{:S(2)}) copy-start(bf16[4,64,192]{1,2,0:T(8,128)(2,1)S(1)} %copy.304) | copy-start | bytes 294916
  126.2 14.6 %copy-start.86 = (f32[4,3,64,64]{2,3,1,0:T(8,128)}, f32[4,3,64,64]{2,3,1,0:T(8,128)S(1)}, u32[]{:S(2)}) copy-start(f32[4,3,64,64]{2,3,1,0:T(8,128)S(1)} %get-tuple-element.219) | copy-start | bytes 589828
  126.2 14.6 %copy-start.128 = (f32[4,3,64]{2,1,0:T(4,128)}, f32[4,3,64]{2,1,0:T(4,128)S(1)}, u32[]{:S(2)}) copy-start(f32[4,3,64]{2,1,0:T(4,128)S(1)} %get-tuple-element.218) | copy-start | bytes 9220
  126.7 14.2 %copy-start.144 = (f32[4,3,64]{2,1,0:T(4,128)}, f32[4,3,64]{2,1,0:T(4,128)S(1)}, u32[]{:S(2)}) copy-start(f32[4,3,64]{2,1,0:T(4,128)S(1)} %fusion.173) | copy-start | bytes 9220
  153.5 14.3 %copy-start.74 = (bf16[4,3,512,64]{2,3,1,0:T(8,128)(2,1)}, bf16[4,3,512,64]{2,3,1,0:T(8,128)(2,1)S(1)}, u32[]{:S(2)}) copy-start(bf16[4,3,512,64]{2,3,1,0:T(8,128)(2,1)S(1)} %fusion.220) | copy-start | bytes 2359300
  171.7 276.6 %all-reduce.12.cloned.1.call-start = ((), (), s32[]{:S(2)}) async-start(), calls=%async_computation.7 | async-start | bytes 6291456 | tf_op jit(solution)/shard_map/psum | solution.py:85
  172.3 125.8 %copy-start.100 = (f32[768]{0:T(1024)}, f32[768]{0:T(1024)S(1)}, u32[]{:S(2)}) copy-start(f32[768]{0:T(1024)S(1)} %convert_element_type.267) | copy-start | bytes 9220
  306.9 15.4 %copy-start.32 = (f32[4,512,768]{2,1,0:T(8,128)}, f32[4,512,768]{2,1,0:T(8,128)S(1)}, u32[]{:S(2)}) copy-start(f32[4,512,768]{2,1,0:T(8,128)S(1)} %get-tuple-element.222) | copy-start | bytes 18874372
  306.9 17.1 %copy-start.216 = (bf16[768,768]{1,0:T(8,128)(2,1)S(1)}, bf16[768,768]{1,0:T(8,128)(2,1)}, u32[]{:S(2)}) copy-start(bf16[768,768]{1,0:T(8,128)(2,1)} %param.24) | copy-start | bytes 3538948
  328.1 184.1 %all-gather.8.cloned.1.call-start = ((), (), s32[]{:S(2)}) async-start(), calls=%async_computation.8 | async-start | bytes 3932160 | tf_op jit(solution)/shard_map/all_gather | solution.py:81
  328.7 329.7 %all-reduce.14.cloned.1.call-start = ((), (), s32[]{:S(2)}) async-start(), calls=%async_computation.9 | async-start | bytes 6291456 | tf_op jit(solution)/shard_map/psum | solution.py:85
  448.3 6.5 copy-start.12
  448.3 6.5 copy-start.101
  448.3 6.5 copy-start.109
  448.3 6.5 copy-start.125
  448.3 6.5 copy-start.127
  512.2 8.9 copy-start.11
  512.2 8.9 copy-start.112
  512.2 8.9 copy-start.116
  523.7 9.0 copy-start.78
  538.5 119.9 %copy-start.102 = (f32[768]{0:T(1024)S(1)}, f32[768]{0:T(1024)}, u32[]{:S(2)}) copy-start(f32[768]{0:T(1024)} %copy-done.100) | copy-start | bytes 9220
  538.5 119.9 %copy-start.110 = (f32[768]{0:T(1024)S(1)}, f32[768]{0:T(1024)}, u32[]{:S(2)}) copy-start(f32[768]{0:T(1024)} %get-tuple-element.134) | copy-start | bytes 9220
  538.5 119.9 %copy-start.113 = (f32[4,512]{1,0:T(4,128)S(1)}, f32[4,512]{1,0:T(4,128)}, u32[]{:S(2)}) copy-start(f32[4,512]{1,0:T(4,128)} %add_rsqrt_fusion) | copy-start | bytes 24580
  538.5 119.9 %copy-start.117 = (f32[768]{0:T(1024)S(1)}, f32[768]{0:T(1024)}, u32[]{:S(2)}) copy-start(f32[768]{0:T(1024)} %get-tuple-element.132) | copy-start | bytes 9220
  538.5 119.9 %copy-start.120 = (f32[4,512]{1,0:T(4,128)S(1)}, f32[4,512]{1,0:T(4,128)}, u32[]{:S(2)}) copy-start(f32[4,512]{1,0:T(4,128)} %copy-done.119) | copy-start | bytes 24580
  538.5 119.9 %copy-start.122 = (f32[4,512]{1,0:T(4,128)S(1)}, f32[4,512]{1,0:T(4,128)}, u32[]{:S(2)}) copy-start(f32[4,512]{1,0:T(4,128)} %copy-done.121) | copy-start | bytes 24580
  538.5 157.9 %all-reduce.16.cloned.1.call-start = ((), (), s32[]{:S(2)}) async-start(), calls=%async_computation.10 | async-start | bytes 393216 | tf_op jit(solution)/shard_map/psum | solution.py:295
  658.4 10.7 %copy-start.4 = (bf16[4,512,768]{2,1,0:T(8,128)(2,1)S(1)}, bf16[4,512,768]{2,1,0:T(8,128)(2,1)}, u32[]{:S(2)}) copy-start(bf16[4,512,768]{2,1,0:T(8,128)(2,1)} %all-gather.6.cloned.1.call-done) | copy-start | bytes 9437188
  658.4 10.7 %copy-start.8 = (bf16[4,512,768]{2,1,0:T(8,128)(2,1)S(1)}, bf16[4,512,768]{2,1,0:T(8,128)(2,1)}, u32[]{:S(2)}) copy-start(bf16[4,512,768]{2,1,0:T(8,128)(2,1)} %all-reduce.10.cloned.1.call-done) | copy-start | bytes 9437188
  679.2 90.7 %all-reduce.20.cloned.1.call-start = ((), (), s32[]{:S(2)}) async-start(), calls=%async_computation.17 | async-start | bytes 786432 | tf_op jit(solution)/shard_map/psum | solution.py:296
  682.5 13.9 %copy-start.43 = (f32[4,3,64,64]{2,3,1,0:T(8,128)S(1)}, f32[4,3,64,64]{2,3,1,0:T(8,128)}, u32[]{:S(2)}) copy-start(f32[4,3,64,64]{2,3,1,0:T(8,128)} %copy-done.42) | copy-start | bytes 589828
  684.3 25.3 %collective-permute-start.2 = (bf16[4,16,192]{1,2,0:T(8,128)(2,1)}, bf16[4,16,192]{1,2,0:T(8,128)(2,1)}, u32[]{:S(2)}, u32[]{:S(2)}) collective-permute-start(bf16[4,16,192]{1,2,0:T(8,128)(2,1)} %get-tuple-element.200), channel_id=1, source_target_pairs={{0,4},{1,5},{2,6},{3,7},{8,12},{9,13},{10,14},{11,15},{16,20},{17,... | collective-permute-start | bytes 73736 | tf_op jit(solution)/shard_map/ppermute | solution.py:35
  686.6 23.0 %collective-permute-start.3 = (bf16[4,16,192]{1,2,0:T(8,128)(2,1)}, bf16[4,16,192]{1,2,0:T(8,128)(2,1)}, u32[]{:S(2)}, u32[]{:S(2)}) collective-permute-start(bf16[4,16,192]{1,2,0:T(8,128)(2,1)} %get-tuple-element.201), channel_id=1, source_target_pairs={{4,0},{5,1},{6,2},{7,3},{12,8},{13,9},{14,10},{15,11},{20,16},{21,... | collective-permute-start | bytes 73736 | tf_op jit(solution)/shard_map/ppermute | solution.py:37
  704.0 166.8 %reduce-scatter.18.cloned.1.call-start = ((), (), s32[]{:S(2)}) async-start(), calls=%async_computation.15 | async-start | bytes 884736
  709.4 163.0 %reduce-scatter.16.cloned.1.call-start = ((), (), s32[]{:S(2)}) async-start(), calls=%async_computation.14 | async-start | bytes 2211840
  751.7 15.2 %copy-start.99 = (f32[4,3,64,64]{3,2,1,0:T(8,128)S(1)}, f32[4,3,64,64]{3,2,1,0:T(8,128)}, u32[]{:S(2)}) copy-start(f32[4,3,64,64]{3,2,1,0:T(8,128)} %fusion.119) | copy-start | bytes 589828
  751.7 15.2 %copy-start.146 = (f32[4,3,64]{2,1,0:T(4,128)S(1)}, f32[4,3,64]{2,1,0:T(4,128)}, u32[]{:S(2)}) copy-start(f32[4,3,64]{2,1,0:T(4,128)} %copy-done.144) | copy-start | bytes 9220
  798.8 104.5 %reduce-scatter.10.cloned.1.call-start = ((), (), s32[]{:S(2)}) async-start(), calls=%async_computation.11 | async-start | bytes 3932160 | tf_op jit(solution)/shard_map/reduce_scatter | solution.py:89
  805.1 144.3 %reduce-scatter.12.cloned.1.call-start = ((), (), s32[]{:S(2)}) async-start(), calls=%async_computation.12 | async-start | bytes 2654208 | tf_op jit(solution)/shard_map/reduce_scatter | solution.py:377
  814.8 180.9 %reduce-scatter.14.cloned.1.call-start = ((), (), s32[]{:S(2)}) async-start(), calls=%async_computation.13 | async-start | bytes 2654208 | tf_op jit(solution)/shard_map/reduce_scatter | solution.py:378
  873.6 122.1 %copy-start.1 = (bf16[768,768]{1,0:T(8,128)(2,1)S(1)}, bf16[768,768]{1,0:T(8,128)(2,1)}, u32[]{:S(2)}) copy-start(bf16[768,768]{1,0:T(8,128)(2,1)} %param.22) | copy-start | bytes 3538948
  (188 other events, 385.0 us)
Sparse Core Ops, SparseCore 0:
  9.6 66.1 all-gather.5
  89.4 18.2 all-reduce.17
  171.8 122.2 all-reduce.9
  328.2 120.0 all-reduce.11
  449.7 62.4 all-gather.7
  538.6 119.6 all-reduce.13
  679.3 17.0 all-reduce.15
  704.1 19.6 all-reduce.19
  727.0 36.1 reduce-scatter.17
  799.0 41.5 reduce-scatter.15
  842.8 60.4 reduce-scatter.9
  907.1 42.2 reduce-scatter.11
  953.3 42.3 reduce-scatter.13
where the time goes:
time: 1010 us; the launch traced here: 1000 us
  waiting for transfers between devices  610 us (60%)
  matrix products  176 us (17%)
  other arithmetic  101 us (10%)
  local copies, waits for them, and re-layouts  55.4 us (5%)
  blocking collectives  34.7 us (3%)
  between operations  17.7 us (2%)
    psum x3, waiting for transfers between devices, sum_rows(): lax.psum(partial_value.astype(jnp.bfloat16), 'head').astype(jnp.float32)  355 us
    all_gather x2, waiting for transfers between devices, gather_rows(): return lax.all_gather(partial_value, 'head', axis=1, tiled=True)  112 us
    reduce_scatter x1, waiting for transfers between devices, on_device(): lax.psum_scatter(w_down_grad, ('row', 'seq'), scatter_dimension=1, tiled=...  46.3 us
    reduce_scatter x1, waiting for transfers between devices, on_device(): lax.psum_scatter(w_hidden_grad, ('row', 'seq'), scatter_dimension=0, tile...  43.4 us
    unnamed x445, local copies, waits for them, and re-layouts  41.6 us
    reduce_scatter x1, waiting for transfers between devices, sum_shares(): lax.psum_scatter(partial_value.astype(jnp.bfloat16), 'head', scatter_dime...  28.8 us
    dot_general x36, matrix products, newton_schulz_inverse(): jnp.einsum('...ij,...jk->...ik', product, nested, precision=HIGH_ACCURACY)  26.8 us
    psum x1, blocking collectives, on_device(): lax.psum((proj_bias_grad, taps_grad, out_bias_grad, norm_attn_grad, hid_b...  25.8 us
  transfers between devices with their start and end apart: 17, of which 10 were waited for; matrix products, arithmetic and copies ran while one was open for 18% of the time, Pallas kernels for 0%

commit v1 on v0

v1 whole, which is shorter than its diff:
```python
import jax
import jax.numpy as jnp
from jax import lax
from jax.sharding import PartitionSpec as P

HEAD_DIM = 64
LANDMARKS = 64
CONV_TAPS = 33
NEWTON_STEPS = 6


EPS = 1e-05
HIGH_ACCURACY = lax.Precision.HIGHEST


def combined_all(part, axis, combine):
    gathered = jax.tree.map(lambda a: lax.all_gather(a, axis), part)

    def take(source):
        return jax.tree.map(lambda a: lax.dynamic_index_in_dim(a, source, 0, False), gathered)

    return lax.fori_loop(
        1, lax.axis_size(axis), lambda source, state: combine(state, take(source)), take(0)
    )


def padded(cells, sides, width):
    for axis, dim in sides:
        count = lax.axis_size(axis)
        ends = count - 1
        head = lax.slice_in_dim(cells, 0, width, axis=dim)
        tail = lax.slice_in_dim(cells, cells.shape[dim] - width, cells.shape[dim], axis=dim)
        cells = jnp.concatenate(
            [
                lax.ppermute(tail, axis, [(i, (i + 1) % count) for i in range(ends)]),
                cells,
                lax.ppermute(head, axis, [((i + 1) % count, i) for i in range(ends)]),
            ],
            axis=dim,
        )
    return cells


def newton_schulz_inverse(kernel):
    order_size = kernel.shape[-1]
    identity = jnp.eye(order_size, dtype=jnp.float32)
    estimate = jnp.swapaxes(kernel, -1, -2) / order_size
    for repeat in range(NEWTON_STEPS):
        product = jnp.einsum("...ij,...jk->...ik", kernel, estimate, precision=HIGH_ACCURACY)
        nested = 7.0 * identity - product
        nested = 15.0 * identity - jnp.einsum(
            "...ij,...jk->...ik", product, nested, precision=HIGH_ACCURACY
        )
        nested = 13.0 * identity - jnp.einsum(
            "...ij,...jk->...ik", product, nested, precision=HIGH_ACCURACY
        )
        estimate = 0.25 * jnp.einsum(
            "...ij,...jk->...ik", estimate, nested, precision=HIGH_ACCURACY
        )
    return estimate


def exact_gelu(pre_act):
    return jax.nn.gelu(pre_act, approximate=False)


def merge_softmax(former, latter):
    top_one, total_one, pooled_one = former
    top_two, total_two, pooled_two = latter
    top_new = jnp.maximum(top_one, top_two)
    factor_one = jnp.exp(top_one - top_new)
    factor_two = jnp.exp(top_two - top_new)
    return (
        top_new,
        total_one * factor_one + total_two * factor_two,
        pooled_one * factor_one[..., None] + pooled_two * factor_two[..., None],
    )


def swap_sum(tree):
    if lax.axis_size("seq") == 2:
        other = jax.tree.map(lambda a: lax.ppermute(a, "seq", [(0, 1), (1, 0)]), tree)
        return jax.tree.map(lambda a, b: a + b, tree, other)
    return lax.psum(tree, "seq")


def swap_merge(part, combine):
    if lax.axis_size("seq") == 2:
        other = jax.tree.map(lambda a: lax.ppermute(a, "seq", [(0, 1), (1, 0)]), part)
        return combine(part, other)
    return combined_all(part, "seq", combine)


def to_documents(rows):
    return lax.all_to_all(rows, "head", split_axis=0, concat_axis=1, tiled=True)


def to_positions(rows):
    return lax.all_to_all(rows, "head", split_axis=1, concat_axis=0, tiled=True)


ALL_AXES = ("head", "row", "seq")


def gather_weight(shard):
    count = lax.axis_size("row") * lax.axis_size("seq")
    place = lax.axis_index("row") * lax.axis_size("seq") + lax.axis_index("seq")
    size = shard.shape[0] // count
    piece = lax.dynamic_slice_in_dim(shard, place * size, size, axis=0)
    return lax.all_gather(piece, ALL_AXES, axis=0, tiled=True)


def scatter_grad(grad):
    shards, features, columns = grad.shape
    low = grad.reshape(shards * features, columns).astype(jnp.bfloat16)
    return lax.psum_scatter(low, ALL_AXES, scatter_dimension=0, tiled=True).astype(jnp.float32)


def norm_apply(residual, gain_row, shift_row):
    former = jnp.mean(residual, axis=-1)
    centered_raw = residual - former[..., None]
    variance = jnp.mean(centered_raw * centered_raw, axis=-1)
    inv_dev = lax.rsqrt(variance + EPS)
    centered = centered_raw * inv_dev[..., None]
    return (centered * gain_row + shift_row, centered, inv_dev)


def norm_back(incoming, centered, inv_dev, gain_row):
    scaled = incoming * gain_row
    former = jnp.mean(scaled, axis=-1)
    latter = jnp.mean(scaled * centered, axis=-1)
    return inv_dev[..., None] * (scaled - former[..., None] - centered * latter[..., None])


def norm_grads(incoming, centered):
    return jnp.stack([jnp.sum(incoming * centered, axis=(0, 1)), jnp.sum(incoming, axis=(0, 1))])


def on_device(
    inputs,
    segment_ids,
    w_project,
    proj_bias,
    conv_taps,
    w_output,
    out_bias,
    norm_attn,
    w_hidden,
    hid_bias,
    w_down,
    down_bias,
    norm_ffn,
    cotangent,
):
    model_width = inputs.shape[2]
    shards = lax.axis_size("head")
    heads_shard = w_project.shape[0]
    heads = heads_shard * shards
    hidden_shard = w_hidden.shape[1]
    width_shard = heads_shard * HEAD_DIM
    half_taps = CONV_TAPS // 2
    scores_factor = HEAD_DIM ** (-0.5)
    head_place = lax.axis_index("head")

    x_rows = to_documents(inputs)
    seqs, tokens, _ = x_rows.shape
    small_pack = jnp.concatenate([proj_bias.reshape(-1), conv_taps.reshape(-1), hid_bias])
    small_all = lax.all_gather(small_pack, "head", axis=0)
    split_one = 2 * width_shard
    split_two = split_one + heads_shard * CONV_TAPS
    bias_all = small_all[:, :split_one].reshape(shards, 2, width_shard)
    bias_all = jnp.swapaxes(bias_all, 0, 1).reshape(2, model_width)
    taps_all = small_all[:, split_one:split_two].reshape(heads, CONV_TAPS)
    hid_all = small_all[:, split_two:].reshape(shards * hidden_shard)

    proj_full = gather_weight(w_project.reshape(-1, model_width)).reshape(
        heads, 3, HEAD_DIM, model_width
    )
    out_full = gather_weight(w_output)
    hidden_full = gather_weight(w_hidden).reshape(shards, model_width, hidden_shard)
    down_full = gather_weight(w_down)
    grad_rows = to_documents(cotangent)

    segment_rows = lax.dynamic_slice_in_dim(segment_ids, head_place * seqs, seqs, axis=0)

    def split_heads(source, row_count):
        return source.reshape(seqs, row_count, heads, HEAD_DIM)

    mixed_proj = jnp.einsum(
        "ste,hcfe->csthf", x_rows, proj_full, preferred_element_type=jnp.float32
    )
    mixed_proj = mixed_proj.reshape(3, seqs, tokens, model_width)
    query_tokens = (mixed_proj[0] + bias_all[0]).astype(jnp.bfloat16)
    key_tokens = mixed_proj[1].astype(jnp.bfloat16)
    value_tokens = (mixed_proj[2] + bias_all[1]).astype(jnp.bfloat16)
    segment_membership = (
        segment_rows[:, :, None] == jnp.arange(LANDMARKS, dtype=jnp.int32)[None, None, :]
    )
    member_low = segment_membership.astype(jnp.bfloat16)
    member_wide = segment_membership.astype(jnp.float32)
    query_sums = jnp.einsum(
        "stm,std->smd", member_low, query_tokens, preferred_element_type=jnp.float32
    )
    key_sums = jnp.einsum(
        "stm,std->smd", member_low, key_tokens, preferred_element_type=jnp.float32
    )
    segment_count = jnp.sum(member_wide, axis=1)
    query_sums, key_sums, segment_count = swap_sum((query_sums, key_sums, segment_count))
    query_landmarks = (query_sums / segment_count[:, :, None]).astype(jnp.bfloat16)
    key_landmarks = (key_sums / segment_count[:, :, None]).astype(jnp.bfloat16)
    q_heads = split_heads(query_tokens, tokens)
    k_heads = split_heads(key_tokens, tokens)
    v_heads = split_heads(value_tokens, tokens)
    ql_heads = split_heads(query_landmarks, LANDMARKS)
    kl_heads = split_heads(key_landmarks, LANDMARKS)
    ql_wide = ql_heads.astype(jnp.float32)
    kl_wide = kl_heads.astype(jnp.float32)
    v_wide = v_heads.astype(jnp.float32)
    first_scores = (
        jnp.einsum("sthd,smhd->shtm", q_heads, kl_heads, preferred_element_type=jnp.float32)
        * scores_factor
    )
    first_kernel = jax.nn.softmax(first_scores, axis=-1)
    kern_low = first_kernel.astype(jnp.bfloat16)
    score_two = (
        jnp.einsum("smhd,snhd->shmn", ql_heads, kl_heads, preferred_element_type=jnp.float32)
        * scores_factor
    )
    second_kernel = jax.nn.softmax(score_two, axis=-1)
    inverse, inverse_back = jax.vjp(newton_schulz_inverse, second_kernel)
    third_scores = (
        jnp.einsum("smhd,sthd->shmt", ql_heads, k_heads, preferred_element_type=jnp.float32)
        * scores_factor
    )
    top_local = jnp.max(third_scores, axis=-1)
    weight_local = jnp.exp(third_scores - top_local[..., None])
    total_local = jnp.sum(weight_local, axis=-1)
    pooled_local = jnp.einsum("shmt,sthd->shmd", weight_local, v_wide, precision=HIGH_ACCURACY)
    top_all, total_all, pooled_all = swap_merge(
        (top_local, total_local, pooled_local), merge_softmax
    )
    segment_means = pooled_all / total_all[..., None]
    log_total = top_all + jnp.log(total_all)
    reduced_mixer = jnp.einsum(
        "shmn,shnd->shmd", inverse, segment_means, precision=HIGH_ACCURACY
    ).astype(jnp.bfloat16)
    landmark_output = jnp.einsum(
        "shtm,shmd->sthd", kern_low, reduced_mixer, preferred_element_type=jnp.float32
    )
    value_rim = padded(value_tokens, (("seq", 1),), half_taps)
    tap_wide = taps_all.astype(jnp.float32)
    band_rows = min(64, tokens)
    band_columns = band_rows + 2 * half_taps
    bands = tokens // band_rows
    offsets = jnp.arange(band_columns)[None, :] - jnp.arange(band_rows)[:, None]
    tap_places = (offsets[None] == jnp.arange(CONV_TAPS)[:, None, None]).astype(jnp.bfloat16)
    back_places = (2 * half_taps - offsets[None] == jnp.arange(CONV_TAPS)[:, None, None]).astype(
        jnp.bfloat16
    )
    toeplitz = jnp.einsum("hj,jpq->hpq", taps_all, tap_places)
    toeplitz_back = jnp.einsum("hj,jpq->hpq", taps_all, back_places)

    def windows(rim):
        return jnp.stack(
            [
                lax.slice_in_dim(rim, i * band_rows, i * band_rows + band_columns, axis=1)
                for i in range(bands)
            ],
            axis=1,
        ).reshape(seqs, bands, band_columns, heads, HEAD_DIM)

    value_windows = windows(value_rim)
    conv_out = jnp.einsum(
        "hpq,sbqhd->sbphd", toeplitz, value_windows, preferred_element_type=jnp.float32
    ).reshape(seqs, tokens, heads, HEAD_DIM)
    attended = (landmark_output + conv_out).reshape(seqs, tokens, model_width).astype(jnp.bfloat16)
    out_part = jnp.dot(attended, out_full, preferred_element_type=jnp.float32)
    gain_one = norm_attn[0].astype(jnp.float32)
    shift_one = norm_attn[1].astype(jnp.float32)
    gain_two = norm_ffn[0].astype(jnp.float32)
    shift_two = norm_ffn[1].astype(jnp.float32)
    resid_one = x_rows.astype(jnp.float32) + out_part + out_bias.astype(jnp.float32)
    normed_one, centered_one, inv_one = norm_apply(resid_one, gain_one, shift_one)
    normed_low = normed_one.astype(jnp.bfloat16)
    hidden_pre = jnp.einsum(
        "ste,gef->stgf", normed_low, hidden_full, preferred_element_type=jnp.float32
    ).reshape(seqs, tokens, shards * hidden_shard) + hid_all.astype(jnp.float32)
    active, gelu_back = jax.vjp(exact_gelu, hidden_pre)
    active_low = active.astype(jnp.bfloat16)
    down_part = jnp.dot(active_low, down_full, preferred_element_type=jnp.float32)
    resid_two = normed_one + down_part + down_bias.astype(jnp.float32)
    normed_two, centered_two, inv_two = norm_apply(resid_two, gain_two, shift_two)
    layer_out = to_positions(normed_two.astype(jnp.bfloat16))
    grad_y = grad_rows.astype(jnp.float32)
    grad_two = norm_back(grad_y, centered_two, inv_two, gain_two)
    norm_ffn_grad = norm_grads(grad_y, centered_two)
    down_low = grad_two.astype(jnp.bfloat16)
    down_bias_grad = jnp.sum(down_low, axis=(0, 1), dtype=jnp.float32)

    def by_shard(source):
        return source.reshape(seqs, tokens, shards, -1)

    w_down_grad = scatter_grad(
        jnp.einsum(
            "stgf,ste->gef", by_shard(active_low), down_low, preferred_element_type=jnp.float32
        )
    )
    grad_active = jnp.einsum("ste,fe->stf", down_low, down_full, preferred_element_type=jnp.float32)
    grad_pre = gelu_back(grad_active)[0].astype(jnp.bfloat16)
    hid_bias_grad = jnp.sum(grad_pre, axis=(0, 1), dtype=jnp.float32)
    w_hidden_grad = scatter_grad(
        jnp.einsum(
            "stgf,ste->gef", by_shard(grad_pre), normed_low, preferred_element_type=jnp.float32
        )
    )
    back_part = jnp.einsum(
        "stgf,gef->ste", by_shard(grad_pre), hidden_full, preferred_element_type=jnp.float32
    )
    grad_in = grad_two + back_part
    grad_one = norm_back(grad_in, centered_one, inv_one, gain_one)
    norm_attn_grad = norm_grads(grad_in, centered_one)
    out_low = grad_one.astype(jnp.bfloat16)
    out_bias_grad = jnp.sum(out_low, axis=(0, 1), dtype=jnp.float32)
    w_output_grad = scatter_grad(
        jnp.einsum(
            "stgd,ste->ged", by_shard(attended), out_low, preferred_element_type=jnp.float32
        )
    )
    grad_att = jnp.einsum(
        "ste,de->std", out_low, out_full, preferred_element_type=jnp.float32
    ).astype(jnp.bfloat16)
    grad_heads = split_heads(grad_att, tokens)
    mixer_part = jnp.einsum(
        "shtm,sthd->shmd", kern_low, grad_heads, preferred_element_type=jnp.float32
    )
    kern_grad = jnp.einsum(
        "sthd,shmd->shtm", grad_heads, reduced_mixer, preferred_element_type=jnp.float32
    )
    score_grad = first_kernel * (
        kern_grad - jnp.sum(first_kernel * kern_grad, axis=-1, keepdims=True)
    )
    score_low = score_grad.astype(jnp.bfloat16)
    query_grad = (
        jnp.einsum("shtm,smhd->sthd", score_low, kl_heads, preferred_element_type=jnp.float32)
        * scores_factor
    )
    kl_part = (
        jnp.einsum("shtm,sthd->smhd", score_low, q_heads, preferred_element_type=jnp.float32)
        * scores_factor
    )
    mixer_grad, kl_grad_one = swap_sum((mixer_part, kl_part))
    inverse_grad = jnp.einsum("shmd,shnd->shmn", mixer_grad, segment_means, precision=HIGH_ACCURACY)
    pooled_grad = jnp.einsum("shmn,shmd->shnd", inverse, mixer_grad, precision=HIGH_ACCURACY)
    kern_two_grad = inverse_back(inverse_grad)[0]
    score_two_grad = second_kernel * (
        kern_two_grad - jnp.sum(second_kernel * kern_two_grad, axis=-1, keepdims=True)
    )
    ql_grad_two = (
        jnp.einsum("shmn,snhd->smhd", score_two_grad, kl_wide, precision=HIGH_ACCURACY)
        * scores_factor
    )
    kl_grad_two = (
        jnp.einsum("shmn,smhd->snhd", score_two_grad, ql_wide, precision=HIGH_ACCURACY)
        * scores_factor
    )
    third_kernel = jnp.exp(third_scores - log_total[..., None])
    kern_three_grad = jnp.einsum("shmd,sthd->shmt", pooled_grad, v_wide, precision=HIGH_ACCURACY)
    row_dot = jnp.sum(pooled_grad * segment_means, axis=-1, keepdims=True)
    score_three_low = (third_kernel * (kern_three_grad - row_dot)).astype(jnp.bfloat16)
    ql_part = (
        jnp.einsum("shmt,sthd->smhd", score_three_low, k_heads, preferred_element_type=jnp.float32)
        * scores_factor
    )
    key_grad = (
        jnp.einsum("shmt,smhd->sthd", score_three_low, ql_heads, preferred_element_type=jnp.float32)
        * scores_factor
    )
    value_grad = jnp.einsum("shmt,shmd->sthd", third_kernel, pooled_grad, precision=HIGH_ACCURACY)
    ql_grad = swap_sum(ql_part) + ql_grad_two
    kl_grad = kl_grad_one + kl_grad_two
    per_count = 1.0 / segment_count[:, :, None]
    ql_spread = ql_grad.reshape(seqs, LANDMARKS, model_width) * per_count
    kl_spread = kl_grad.reshape(seqs, LANDMARKS, model_width) * per_count
    query_grad = query_grad + split_heads(
        jnp.einsum("stm,smd->std", member_wide, ql_spread, precision=HIGH_ACCURACY), tokens
    )
    key_grad = key_grad + split_heads(
        jnp.einsum("stm,smd->std", member_wide, kl_spread, precision=HIGH_ACCURACY), tokens
    )
    grad_windows = windows(padded(grad_att, (("seq", 1),), half_taps))
    value_grad = value_grad + jnp.einsum(
        "hpq,sbqhd->sbphd", toeplitz_back, grad_windows, preferred_element_type=jnp.float32
    ).reshape(seqs, tokens, heads, HEAD_DIM)
    band_sums = jnp.einsum(
        "sbphd,sbqhd->hpq",
        grad_att.reshape(seqs, bands, band_rows, heads, HEAD_DIM),
        value_windows,
        preferred_element_type=jnp.float32,
    )
    skewed = jnp.pad(band_sums.reshape(heads, band_rows * band_columns), ((0, 0), (0, band_rows)))
    taps_grad = jnp.sum(skewed.reshape(heads, band_rows, band_columns + 1), axis=1)[:, :CONV_TAPS]
    grads_qkv = jnp.stack([query_grad, key_grad, value_grad], axis=3).astype(jnp.bfloat16)
    proj_bias_grad = jnp.sum(grads_qkv[:, :, :, 0::2], axis=(0, 1), dtype=jnp.float32)
    proj_bias_grad = jnp.swapaxes(proj_bias_grad, 0, 1).reshape(2, model_width)
    w_project_grad = scatter_grad(
        jnp.einsum(
            "stgr,ste->ger", by_shard(grads_qkv), x_rows, preferred_element_type=jnp.float32
        )
    )
    input_part = jnp.einsum(
        "sthcf,hcfe->ste", grads_qkv, proj_full, preferred_element_type=jnp.float32
    )
    input_grad = to_positions((input_part + grad_one).astype(jnp.bfloat16))
    small_list = [
        proj_bias_grad,
        taps_grad,
        out_bias_grad,
        norm_attn_grad,
        hid_bias_grad,
        down_bias_grad,
        norm_ffn_grad,
    ]
    small_sum = lax.psum(
        jnp.concatenate([part.reshape(-1) for part in small_list]), ("row", "seq", "head")
    )
    outs, start_at = [], 0
    for part in small_list:
        outs.append(small_sum[start_at : start_at + part.size].reshape(part.shape))
        start_at += part.size

    def own_share(source, axis):
        size = source.shape[axis] // shards
        return lax.dynamic_slice_in_dim(source, head_place * size, size, axis=axis)

    return (
        layer_out,
        input_grad,
        w_project_grad.T.reshape(heads_shard, 3, HEAD_DIM, -1),
        own_share(outs[0], 1),
        own_share(outs[1], 0),
        w_output_grad.T,
        own_share(outs[2], 0),
        own_share(outs[3], 1),
        w_hidden_grad,
        own_share(outs[4], 0),
        w_down_grad.T,
        own_share(outs[5], 0),
        own_share(outs[6], 1),
    )


def solution(mesh):
    in_specs = (
        P("row", ("seq", "head"), None),
        P("row", "seq"),
        P("head", None, None, None),
        P(None, "head"),
        P("head", None),
        P("head", None),
        P(),
        P(),
        P(None, "head"),
        P("head"),
        P("head", None),
        P(),
        P(),
        P("row", ("seq", "head"), None),
    )
    out_specs = (
        P("row", ("seq", "head"), None),
        P("row", ("seq", "head"), None),
        P("head", None, None, ("row", "seq")),
        P(None, "head"),
        P("head", None),
        P("head", ("row", "seq")),
        P("head"),
        P(None, "head"),
        P(("row", "seq"), "head"),
        P("head"),
        P("head", ("row", "seq")),
        P("head"),
        P(None, "head"),
    )
    return jax.shard_map(
        on_device, mesh=mesh, in_specs=in_specs, out_specs=out_specs, check_vma=False
    )
```

time: 1010 us -> 785 us (0.78)
  waiting for transfers between devices: 610 us -> 326 us
  other arithmetic: 101 us -> 40.5 us
  local copies, waits for them, and re-layouts: 55.4 us -> 114 us
  blocking collectives: 34.7 us -> 67.5 us
  starting transfers between devices: 7.69 us -> 30.4 us
    psum x6 -> x0, waiting for transfers between devices: 378 us -> none  [the longest x3 355 us: sum_rows(): lax.psum(partial_value.astype(jnp.bfloat16), 'head').astype(jnp.float32)]
    reduce_scatter x3 -> x2, waiting for transfers between devices: 119 us -> 209 us  [scatter_grad(): lax.psum_scatter(low, ALL_AXES, scatter_dimension=0, tiled=True)]
    all_to_all x0 -> x4, waiting for transfers between devices: none -> 29.2 us  [the longest x2 23 us: to_documents(): return lax.all_to_all(rows, 'head', split_axis=0, concat_axis=1, tiled=True)]
    convert_element_type x14 -> x8, other arithmetic: 33.1 us -> 4.07 us  [the longest x1 1.64 us: scatter_grad(): lax.psum_scatter(low, ALL_AXES, scatter_dimension=0, tiled=True)]
    unnamed x0 -> x1, blocking collectives: none -> 26.7 us
    dot_general x12 -> x17, matrix products: 62.1 us -> 86.9 us  [the longest x1 22.6 us: on_device(): jnp.einsum('ste,gef->stgf', normed_low, hidden_full, preferred_element_ty...]
    all_gather x2 -> x4, waiting for transfers between devices: 112 us -> 87.9 us  [gather_weight(): return lax.all_gather(piece, ALL_AXES, axis=0, tiled=True)]
    reduce_sum x5 -> x3, other arithmetic: 23.8 us -> 1.19 us  [the longest x1 0.86 us: norm_grads(): jnp.sum(incoming, axis=(0, 1))]
  transfers between devices with their start and end apart: 17 -> 25, of which waited for: 10 -> 8; matrix products, arithmetic and copies ran while one was open for 18% -> 35% of each run, Pallas kernels for 0% -> 0%
where the time goes in v1:
time: 785 us; the launch traced here: 775 us
  waiting for transfers between devices  326 us (42%)
  matrix products  178 us (23%)
  local copies, waits for them, and re-layouts  114 us (15%)
  blocking collectives  67.5 us (9%)
  other arithmetic  40.5 us (5%)
  starting transfers between devices  30.4 us (4%)
  between operations  17.6 us (2%)
    reduce_scatter x2, waiting for transfers between devices, scatter_grad(): lax.psum_scatter(low, ALL_AXES, scatter_dimension=0, tiled=True)  209 us
    all_gather x4, waiting for transfers between devices, gather_weight(): return lax.all_gather(piece, ALL_AXES, axis=0, tiled=True)  87.9 us
    unnamed x286, local copies, waits for them, and re-layouts  44.4 us
    psum x1, blocking collectives, on_device(): lax.psum(jnp.concatenate([part.reshape(-1) for part in small_list]), ('ro...  40.7 us
    unnamed x1, blocking collectives  26.7 us
    dot_general x36, matrix products, newton_schulz_inverse(): jnp.einsum('...ij,...jk->...ik', product, nested, precision=HIGH_ACCURACY)  24.9 us
    all_to_all x2, waiting for transfers between devices, to_documents(): return lax.all_to_all(rows, 'head', split_axis=0, concat_axis=1, tiled=True)  23 us
    dot_general x1, matrix products, on_device(): jnp.einsum('ste,gef->stgf', normed_low, hidden_full, preferred_element_ty...  22.6 us
  transfers between devices with their start and end apart: 25, of which 8 were waited for; matrix products, arithmetic and copies ran while one was open for 35% of the time, Pallas kernels for 0%

profile of v1, /device:TPU:0, one launch (start us, length us, event | category | flops | bytes accessed | tf_op | source)
XLA Modules:
  0.0 775.0 jit_solution(18211713082322431543)
XLA Ops:
  11.2 6.4 all-to-all-start.2
  21.9 26.7 %all-reduce.1 = bf16[5004]{0:T(1024)(128)(2,1)S(1)} all-reduce(bf16[5004]{0:T(1024)(128)(2,1)S(1)} %dynamic-update-slice), channel_id=2, replica_groups=mesh['row'=4,'seq'=2,'head'=4] {'head'}, use_global_device_ids=true, to_apply=%add.1 | all-reduce | flops 5004 | bytes 20016
  50.5 3.5 all-to-all-start
  59.3 23.0 %all-to-all-done = bf16[4,128,768]{2,1,0:T(8,128)(2,1)S(1)} async-done(((bf16[4,128,768]{2,1,0:T(8,128)(2,1)}), bf16[4,128,768]{2,1,0:T(8,128)(2,1)S(1)}, u32[]{:S(2)}, u32[]{:S(2)}) %all-to-all-start) | async-done | bytes 786464 | tf_op jit(solution)/shard_map/all_to_all | solution.py:95
  83.8 4.2 convolution_bitcast_fusion
  99.2 3.9 copy.557
  103.2 4.2 reshape.1569
  107.7 2.6 fusion.270
  112.5 3.3 fusion.58
  137.8 2.2 fusion.271
  145.5 4.0 fusion.34
  149.5 2.7 fusion.272
  154.3 50.9 %all-gather.10.cloned.1.call-done = bf16[3072,768]{1,0:T(8,128)(2,1)} async-done(((bf16[96,768]{1,0:T(8,128)(2,1)}), bf16[3072,768]{1,0:T(8,128)(2,1)}) %all-gather.10.cloned.1.call-update) | async-done | bytes 4718608 | tf_op jit(solution)/shard_map/all_gather | solution.py:110
  205.2 6.7 copy.558
  211.8 22.6 %multiply_convert_fusion = (bf16[512,3072]{1,0:T(8,128)(2,1)}, f32[512,3072]{1,0:T(8,128)}, f32[512,3072]{1,0:T(8,128)}) fusion(f32[3072]{0:T(1024)} %reshape.1620, bf16[3072,768]{1,0:T(8,128)(2,1)} %bitcast.773, f32[512,768]{1,0:T(8,128)} %copy-done.15, f32[768]{0:T(1024)} %get-tuple-element.26, f32[768]{0:T(1024)} %get-tuple-element.25, ...), kind=kOutput, calls=%fused_computation.5 | convolution fusion | flops 2521694208 | bytes 22042624 | tf_op jit(solution)/shard_map/ste,gef->stgf/dot_general | solution.py:285
  234.4 35.5 %all-gather.12.cloned.1.call-done = bf16[3072,768]{1,0:T(8,128)(2,1)} async-done(((bf16[96,768]{1,0:T(8,128)(2,1)}), bf16[3072,768]{1,0:T(8,128)(2,1)}) %all-gather.12.cloned.1.call-update) | async-done | bytes 4718608 | tf_op jit(solution)/shard_map/all_gather | solution.py:110
  269.9 6.6 fusion.273
  281.1 10.4 %convert_reduce_fusion = (f32[3072]{0:T(1024)}, bf16[512,3072]{1,0:T(8,128)(2,1)}) fusion(f32[512,3072]{1,0:T(8,128)} %get-tuple-element.34, bf16[3072,768]{1,0:T(8,128)(2,1)S(1)} %copy-done.123, f32[512,768]{1,0:T(8,128)S(1)} %get-tuple-element.28, f32[512,3072]{1,0:T(8,128)} %get-tuple-element.79, f32[3072]{0:T(1024)S(1)} %copy-done.109), kind=kOutput, calls=%fused_computation.3 | convolution fusion | flops 2443047936 | bytes 22044672 | tf_op jit(solution)/shard_map/ste,fe->stf/dot_general | solution.py:308
  291.6 5.6 multiply_reduce_fusion
  301.2 2.3 copy.561
  308.2 2.6 fusion.91
  310.8 3.5 convolution_bitcast_fusion.15
  314.3 2.4 fusion.226
  318.7 2.8 collective-permute-start.11
  323.8 2.5 copy.731
  326.5 2.4 pad_maximum_fusion.3
  355.2 3.8 copy.637
  359.1 3.9 reshape.1601
  407.5 2.5 multiply_convert_fusion.1
  413.7 2.6 fusion.31
  423.7 3.8 convert_bitcast_fusion
  427.4 5.9 copy.730
  434.1 7.4 fusion.16
  441.8 7.3 fusion.19
  450.3 2.2 reshape.1647
  452.6 3.5 copy.775
  456.7 6.4 reduce.63
  464.1 4.5 all-to-all-start.1
  468.5 3.6 fusion.85
  476.7 5.0 fusion.62
  481.7 2.4 copy.774
  484.1 6.4 reduce.64
  491.5 6.2 all-to-all-done.1
  497.7 3.5 all-to-all-start.3
  501.7 40.7 %psum.7 = f32[9612]{0:T(1024)S(1)} all-reduce(f32[9612]{0:T(1024)S(1)} %concatenate.38), channel_id=1, replica_groups=mesh['row'=4,'seq'=2,'head'=4] {'row','seq','head'}, use_global_device_ids=true, to_apply=%region_28.29 | all-reduce | flops 9612 | bytes 76896 | tf_op jit(solution)/shard_map/psum | solution.py:423
  547.2 2.4 reshape.1660
  555.8 98.1 %reduce-scatter.9.cloned.1.call-done = bf16[96,768]{1,0:T(8,128)(2,1)} async-done(((bf16[3072,768]{1,0:T(8,128)(2,1)}), bf16[96,768]{1,0:T(8,128)(2,1)}) %reduce-scatter.9.cloned.1.call-update) | async-done | bytes 147472 | tf_op jit(solution)/shard_map/reduce_scatter | solution.py:116
  655.5 110.6 %reduce-scatter.11.cloned.1.call-done = bf16[96,768]{1,0:T(8,128)(2,1)} async-done(((bf16[3072,768]{1,0:T(8,128)(2,1)}), bf16[96,768]{1,0:T(8,128)(2,1)}) %reduce-scatter.11.cloned.1.call-update) | async-done | bytes 147472 | tf_op jit(solution)/shard_map/reduce_scatter | solution.py:116
  (537 shorter events, 181.3 us)
Async XLA Ops:
  7.2 13.1 %copy-start.126 = (u32[32]{0:T(128)S(1)}, u32[32]{0:T(128)}, u32[]{:S(2)}) copy-start(u32[32]{0:T(128)} %constant.146) | copy-start | bytes 388
  7.2 12.9 %copy-start.122 = (bf16[2,192]{1,0:T(2,128)(2,1)S(1)}, bf16[2,192]{1,0:T(2,128)(2,1)}, u32[]{:S(2)}) copy-start(bf16[2,192]{1,0:T(2,128)(2,1)} %param.17) | copy-start | bytes 2308
  7.2 13.0 %copy-start.125 = (bf16[3,33]{1,0:T(4,128)(2,1)S(1)}, bf16[3,33]{1,0:T(4,128)(2,1)}, u32[]{:S(2)}) copy-start(bf16[3,33]{1,0:T(4,128)(2,1)} %param.18) | copy-start | bytes 598
  7.2 14.3 %copy-start.120 = (bf16[768]{0:T(1024)(128)(2,1)S(1)}, bf16[768]{0:T(1024)(128)(2,1)}, u32[]{:S(2)}) copy-start(bf16[768]{0:T(1024)(128)(2,1)} %param.23) | copy-start | bytes 4612
  7.2 76.6 %all-gather.6.cloned.1.call-start = ((), (), s32[]{:S(2)}) async-start(), calls=%async_computation.8 | async-start | bytes 3649536 | tf_op jit(solution)/shard_map/all_gather | solution.py:110
  7.3 42.0 %copy-start.107 = (bf16[2,768]{1,0:T(2,128)(2,1)S(1)}, bf16[2,768]{1,0:T(2,128)(2,1)}, u32[]{:S(2)}) copy-start(bf16[2,768]{1,0:T(2,128)(2,1)} %param.21) | copy-start | bytes 9220
  8.9 41.0 %copy-start.108 = (bf16[2,768]{1,0:T(2,128)(2,1)S(1)}, bf16[2,768]{1,0:T(2,128)(2,1)}, u32[]{:S(2)}) copy-start(bf16[2,768]{1,0:T(2,128)(2,1)} %param.26) | copy-start | bytes 9220
  9.0 140.5 %all-gather.8.cloned.1.call-start = ((), (), s32[]{:S(2)}) async-start(), calls=%async_computation.9 | async-start | bytes 1216512 | tf_op jit(solution)/shard_map/all_gather | solution.py:110
  10.4 194.7 %all-gather.10.cloned.1.call-start = ((), (), s32[]{:S(2)}) async-start(), calls=%async_computation.10 | async-start | bytes 4866048 | tf_op jit(solution)/shard_map/all_gather | solution.py:110
  11.2 39.3 %all-to-all-start.2 = ((bf16[4,128,768]{2,1,0:T(8,128)(2,1)}), bf16[4,128,768]{2,1,0:T(8,128)(2,1)S(1)}, u32[]{:S(2)}, u32[]{:S(2)}) async-start(bf16[4,128,768]{2,1,0:T(8,128)(2,1)} %param.27), calls=%async_computation.2 | async-start | bytes 1572864 | tf_op jit(solution)/shard_map/all_to_all | solution.py:95
  17.6 38.0 %copy-start.118 = (bf16[768]{0:T(1024)(128)(2,1)S(1)}, bf16[768]{0:T(1024)(128)(2,1)}, u32[]{:S(2)}) copy-start(bf16[768]{0:T(1024)(128)(2,1)} %param.20) | copy-start | bytes 4612
  17.6 39.2 %copy-start.119 = (bf16[768]{0:T(1024)(128)(2,1)S(1)}, bf16[768]{0:T(1024)(128)(2,1)}, u32[]{:S(2)}) copy-start(bf16[768]{0:T(1024)(128)(2,1)} %param.25) | copy-start | bytes 4612
  17.6 252.3 %all-gather.12.cloned.1.call-start = ((), (), s32[]{:S(2)}) async-start(), calls=%async_computation.11 | async-start | bytes 4866048 | tf_op jit(solution)/shard_map/all_gather | solution.py:110
  18.3 76.3 %copy-start.93 = (s32[1,512]{1,0:T(1,128)}, s32[1,512]{1,0:T(1,128)S(1)}, u32[]{:S(2)}) copy-start(s32[1,512]{1,0:T(1,128)S(1)} %constant_dynamic-slice_fusion.8) | copy-start | bytes 6148
  18.4 38.9 %collective-permute-start.1 = (f32[1,64]{1,0:T(1,128)S(1)}, f32[1,64]{1,0:T(1,128)S(1)}, u32[]{:S(2)}, u32[]{:S(2)}) collective-permute-start(f32[1,64]{1,0:T(1,128)S(1)} %bitcast.820), channel_id=1, source_target_pairs={{0,4},{4,0},{1,5},{5,1},{2,6},{6,2},{3,7},{7,3},{8,12},{12,8},{9,1... | collective-permute-start | bytes 776 | tf_op jit(solution)/shard_map/ppermute | solution.py:82
  49.0 63.5 %copy-start.91 = (f32[12,64]{1,0:T(8,128)}, f32[12,64]{1,0:T(8,128)S(1)}, u32[]{:S(2)}) copy-start(f32[12,64]{1,0:T(8,128)S(1)} %reshape.1616) | copy-start | bytes 9220
  49.1 39.1 %copy-start.86 = (f32[12,64]{1,0:T(8,128)}, f32[12,64]{1,0:T(8,128)S(1)}, u32[]{:S(2)}) copy-start(f32[12,64]{1,0:T(8,128)S(1)} %reshape.1615) | copy-start | bytes 9220
  49.2 68.7 %copy-start.34 = (f32[64,64]{1,0:T(8,128)}, f32[64,64]{1,0:T(8,128)S(1)}, u32[]{:S(2)}) copy-start(f32[64,64]{1,0:T(8,128)S(1)} %fusion.215) | copy-start | bytes 49156
  49.2 68.7 %copy-start.76 = (f32[64,64]{1,0:T(8,128)}, f32[64,64]{1,0:T(8,128)S(1)}, u32[]{:S(2)}) copy-start(f32[64,64]{1,0:T(8,128)S(1)} %fusion.216) | copy-start | bytes 49156
  49.2 69.2 %copy-start.74 = (f32[64,64]{1,0:T(8,128)}, f32[64,64]{1,0:T(8,128)S(1)}, u32[]{:S(2)}) copy-start(f32[64,64]{1,0:T(8,128)S(1)} %fusion.217) | copy-start | bytes 49156
  50.5 37.5 %copy-start.96 = (f32[768]{0:T(1024)}, f32[768]{0:T(1024)S(1)}, u32[]{:S(2)}) copy-start(f32[768]{0:T(1024)S(1)} %get-tuple-element.23) | copy-start | bytes 9220
  50.5 37.5 %copy-start.10 = (bf16[4,128,768]{2,1,0:T(8,128)(2,1)}, bf16[4,128,768]{2,1,0:T(8,128)(2,1)S(1)}, u32[]{:S(2)}) copy-start(bf16[4,128,768]{2,1,0:T(8,128)(2,1)S(1)} %all-to-all-done.2) | copy-start | bytes 2359300
  50.5 31.7 %all-to-all-start = ((bf16[4,128,768]{2,1,0:T(8,128)(2,1)}), bf16[4,128,768]{2,1,0:T(8,128)(2,1)S(1)}, u32[]{:S(2)}, u32[]{:S(2)}) async-start(bf16[4,128,768]{2,1,0:T(8,128)(2,1)} %param.14), calls=%async_computation | async-start | bytes 1572864 | tf_op jit(solution)/shard_map/all_to_all | solution.py:95
  54.0 498.4 %reduce-scatter.15.cloned.1.call-start = ((), (), s32[]{:S(2)}) async-start(), calls=%async_computation.15 | async-start | bytes 1622016
  90.5 16.8 %collective-permute-start = (f32[1,64,768]{2,1,0:T(8,128)S(1)}, f32[1,64,768]{2,1,0:T(8,128)S(1)}, u32[]{:S(2)}, u32[]{:S(2)}) collective-permute-start(f32[1,64,768]{2,1,0:T(8,128)S(1)} %convolution_bitcast_fusion.17), channel_id=1, source_target_pairs={{0,4},{4,0},{1,5},{5,1},{2,6},{6,2},{3,7},{7,3},{8,12},{12,8},{9,1... | collective-permute-start | bytes 589832 | tf_op jit(solution)/shard_map/ppermute | solution.py:82
  91.1 5.1 collective-permute-start.6
  93.3 3.3 collective-permute-start.7
  95.0 12.4 %collective-permute-start.2 = (f32[1,64,768]{2,1,0:T(8,128)S(1)}, f32[1,64,768]{2,1,0:T(8,128)S(1)}, u32[]{:S(2)}, u32[]{:S(2)}) collective-permute-start(f32[1,64,768]{2,1,0:T(8,128)S(1)} %convolution_bitcast_fusion.16), channel_id=1, source_target_pairs={{0,4},{4,0},{1,5},{5,1},{2,6},{6,2},{3,7},{7,3},{8,12},{12,8},{9,1... | collective-permute-start | bytes 589832 | tf_op jit(solution)/shard_map/ppermute | solution.py:82
  112.0 28.6 %collective-permute-start.5 = (f32[1,12,64]{2,1,0:T(8,128)}, f32[1,12,64]{2,1,0:T(8,128)}, u32[]{:S(2)}, u32[]{:S(2)}) collective-permute-start(f32[1,12,64]{2,1,0:T(8,128)} %bitcast.29), channel_id=1, source_target_pairs={{0,4},{4,0},{1,5},{5,1},{2,6},{6,2},{3,7},{7,3},{8,12},{12,8},{9,1... | collective-permute-start | bytes 9224 | tf_op jit(solution)/shard_map/ppermute | solution.py:89
  112.1 28.5 %collective-permute-start.3 = (f32[1,12,64]{2,1,0:T(8,128)}, f32[1,12,64]{2,1,0:T(8,128)}, u32[]{:S(2)}, u32[]{:S(2)}) collective-permute-start(f32[1,12,64]{2,1,0:T(8,128)} %bitcast.24), channel_id=1, source_target_pairs={{0,4},{4,0},{1,5},{5,1},{2,6},{6,2},{3,7},{7,3},{8,12},{12,8},{9,1... | collective-permute-start | bytes 9224 | tf_op jit(solution)/shard_map/ppermute | solution.py:89
  115.8 26.3 %collective-permute-start.4 = (f32[1,12,64,64]{2,3,1,0:T(8,128)}, f32[1,12,64,64]{2,3,1,0:T(8,128)}, u32[]{:S(2)}, u32[]{:S(2)}) collective-permute-start(f32[1,12,64,64]{2,3,1,0:T(8,128)} %bitcast.27), channel_id=1, source_target_pairs={{0,4},{4,0},{1,5},{5,1},{2,6},{6,2},{3,7},{7,3},{8,12},{12,8},{9,1... | collective-permute-start | bytes 589832 | tf_op jit(solution)/shard_map/ppermute | solution.py:89
  269.9 11.2 %copy-start.123 = (bf16[3072,768]{1,0:T(8,128)(2,1)S(1)}, bf16[3072,768]{1,0:T(8,128)(2,1)}, u32[]{:S(2)}) copy-start(bf16[3072,768]{1,0:T(8,128)(2,1)} %all-gather.12.cloned.1.call-done) | copy-start | bytes 14155780
  278.9 12.6 %slice-start = ((s8[4718592]{0:T(1024)(128)(4,1)}), s8[4194304]{0:T(1024)(128)(4,1)S(1)}, s32[]{:S(2)}) async-start(s8[4718592]{0:T(1024)(128)(4,1)} %bitcast.768), calls=%async_computation.16 | async-start | bytes 8388608
  281.1 10.4 %copy-start.78 = (f32[512,768]{1,0:T(8,128)}, f32[512,768]{1,0:T(8,128)S(1)}, u32[]{:S(2)}) copy-start(f32[512,768]{1,0:T(8,128)S(1)} %get-tuple-element.28) | copy-start | bytes 4718596
  281.1 10.4 %copy-start.16 = (f32[512,768]{1,0:T(8,128)S(1)}, f32[512,768]{1,0:T(8,128)}, u32[]{:S(2)}) copy-start(f32[512,768]{1,0:T(8,128)} %copy-done.15) | copy-start | bytes 4718596
  281.1 10.4 %slice-start.1 = ((s8[4718592]{0:T(1024)(128)(4,1)}), s8[524288]{0:T(1024)(128)(4,1)S(1)}, s32[]{:S(2)}) async-start(s8[4718592]{0:T(1024)(128)(4,1)} %bitcast.768), calls=%async_computation.17 | async-start | bytes 1048576
  316.7 84.6 %collective-permute-start.10 = (f32[1,64,12,64]{3,1,2,0:T(8,128)}, f32[1,64,12,64]{3,1,2,0:T(8,128)}, u32[]{:S(2)}, u32[]{:S(2)}) collective-permute-start(f32[1,64,12,64]{3,1,2,0:T(8,128)} %fusion.91), channel_id=1, source_target_pairs={{0,4},{4,0},{1,5},{5,1},{2,6},{6,2},{3,7},{7,3},{8,12},{12,8},{9,1... | collective-permute-start | bytes 589832 | tf_op jit(solution)/shard_map/ppermute | solution.py:82
  317.0 46.0 %collective-permute-start.8 = (f32[1,12,64,64]{3,2,1,0:T(8,128)}, f32[1,12,64,64]{3,2,1,0:T(8,128)}, u32[]{:S(2)}, u32[]{:S(2)}) collective-permute-start(f32[1,12,64,64]{3,2,1,0:T(8,128)} %convolution_bitcast_fusion.15), channel_id=1, source_target_pairs={{0,4},{4,0},{1,5},{5,1},{2,6},{6,2},{3,7},{7,3},{8,12},{12,8},{9,1... | collective-permute-start | bytes 589832 | tf_op jit(solution)/shard_map/ppermute | solution.py:82
  318.7 7.8 %collective-permute-start.11 = (bf16[1,16,768]{2,1,0:T(8,128)(2,1)}, bf16[1,16,768]{2,1,0:T(8,128)(2,1)}, u32[]{:S(2)}, u32[]{:S(2)}) collective-permute-start(bf16[1,16,768]{2,1,0:T(8,128)(2,1)} %get-tuple-element.47), channel_id=1, source_target_pairs={{0,4},{1,5},{2,6},{3,7},{8,12},{9,13},{10,14},{11,15},{16,20},{17,... | collective-permute-start | bytes 73736 | tf_op jit(solution)/shard_map/ppermute | solution.py:35
  321.4 5.0 collective-permute-start.12
  326.4 227.6 %reduce-scatter.13.cloned.1.call-start = ((), (), s32[]{:S(2)}) async-start(), calls=%async_computation.14 | async-start | bytes 4055040
  412.0 5.8 collective-permute-start.9
  433.4 220.4 %reduce-scatter.9.cloned.1.call-start = ((), (), s32[]{:S(2)}) async-start(), calls=%async_computation.12 | async-start | bytes 4866048 | tf_op jit(solution)/shard_map/reduce_scatter | solution.py:116
  441.5 324.6 %reduce-scatter.11.cloned.1.call-start = ((), (), s32[]{:S(2)}) async-start(), calls=%async_computation.13 | async-start | bytes 4866048 | tf_op jit(solution)/shard_map/reduce_scatter | solution.py:116
  464.1 33.6 %all-to-all-start.1 = ((bf16[4,2,49152]{2,1,0:T(2,128)(2,1)}), bf16[4,2,49152]{2,1,0:T(2,128)(2,1)}, u32[]{:S(2)}, u32[]{:S(2)}) async-start(bf16[4,2,49152]{2,1,0:T(2,128)(2,1)} %reshape.1659), calls=%async_computation.1 | async-start | bytes 1572864 | tf_op jit(solution)/shard_map/all_to_all | solution.py:99
  490.5 10.7 %copy-start.110 = (f32[1,768]{1,0:T(1,128)S(1)}, f32[1,768]{1,0:T(1,128)}, u32[]{:S(2)}) copy-start(f32[1,768]{1,0:T(1,128)} %stack.122) | copy-start | bytes 9220
  497.7 53.0 %all-to-all-start.3 = ((bf16[4,2,49152]{2,1,0:T(2,128)(2,1)}), bf16[4,2,49152]{2,1,0:T(2,128)(2,1)S(1)}, u32[]{:S(2)}, u32[]{:S(2)}) async-start(bf16[4,2,49152]{2,1,0:T(2,128)(2,1)} %reshape.1661), calls=%async_computation.3 | async-start | bytes 1572864 | tf_op jit(solution)/shard_map/all_to_all | solution.py:99
  551.4 216.3 %copy-start.1 = (bf16[768,768]{1,0:T(8,128)(2,1)S(1)}, bf16[768,768]{1,0:T(8,128)(2,1)}, u32[]{:S(2)}) copy-start(bf16[768,768]{1,0:T(8,128)(2,1)} %param.22) | copy-start | bytes 3538948
  (106 other events, 285.3 us)
Sparse Core Ops, SparseCore 0:
  11.5 72.2 all-gather.5
  87.3 52.3 all-gather.7
  142.6 62.4 all-gather.9
  207.9 61.9 all-gather.11
  326.5 97.5 reduce-scatter.14
  433.5 108.3 reduce-scatter.12
  547.3 106.4 reduce-scatter.8
  659.3 106.7 reduce-scatter.10
